TPU v7x, 256 devices: a whole 4x4x8 slice. The times are simulated.
256 devices in a mesh: row: 64 (over x, z_hi, y), col: 4 (over z_lo, core).
Axes of the slice: x: 4, y: 4, z: 8 (z_hi: 4, z_lo: 2; z = z_hi * 2 + z_lo), core: 2. Of those that a mesh axis runs over, the one named last changes fastest.
Arguments:
- features: bfloat16 [512, 512, 256], P('row', 'col'), may hold values from -6 to 6
- target: bfloat16 [512, 512, 256], P('row', 'col'), may hold values from -6 to 6
- hole_mask: int32 [512, 512], P('row', 'col'), may hold values 0 or 1
- kernel_first: bfloat16 [3, 3, 256, 256], replicated, may hold values from -0.125 to 0.125
- kernel_second: bfloat16 [3, 3, 256, 256], replicated, may hold values from -0.125 to 0.125
- inputs: bfloat16 [512, 512, 512], P(('row', 'col')), may hold values from -6 to 6
- weight_in: bfloat16 [512, 192], replicated, may hold values from -0.25 to 0.25
- weight_out: bfloat16 [192, 256], replicated, may hold values from -0.4375 to 0.4375
- weight_local: bfloat16 [512, 256], replicated, may hold values from -0.25 to 0.25
- weight_mix: bfloat16 [384, 384], replicated, may hold values from -0.3125 to 0.3125
Outputs:
- grad_inputs: bfloat16 [512, 512, 512], P(('row', 'col'))
Inputs may be any that keep to these rules, and one draw needn't show every extreme that they name: `hole_mask`: 1 marks a pixel to be filled.
All inputs are finite; a program needn't handle non-finite values. No bound on the sum of `hole_mask` on one device may be relied on, other than what follows from the above.
Results may differ from a plain program's by a relative error of at most 0.0095.
Values may be sent and summed in bfloat16 or wider, within the bound.
A program may use at most 64 MiB of HBM per device.

v0:
```python
import functools
import math

import jax
import jax.numpy as jnp
import numpy as np
from jax import lax
from jax.experimental import pallas as pl
from jax.experimental.pallas import tpu as pltpu
from jax.sharding import PartitionSpec as P

MESH = pl.DeviceIdType.MESH
SIDES = [(-1, 0), (1, 0), (-1, -1), (-1, 1), (1, -1), (1, 1), (0, -1), (0, 1)]


def host_tables(length):
    ids = np.arange(length, dtype=np.int64)
    angles = (2.0 * np.pi / length) * ((ids[:, None] * ids[None, :]) % length)
    return (np.cos(angles).astype(jnp.bfloat16), np.sin(angles).astype(jnp.bfloat16))


def dot(left, right):
    return jnp.dot(left, right, preferred_element_type=jnp.float32)


def dot_t(left, right):
    return lax.dot_general(left, right, (((1,), (1,)), ((), ())), preferred_element_type=jnp.float32)


def ids(shape, dim):
    return lax.broadcasted_iota(jnp.int32, shape, dim)


def ones_where(condition):
    return jnp.where(condition, 1.0, 0.0).astype(jnp.bfloat16)


def block_kernel(
    sizes,
    features_any,
    target_any,
    mask_any,
    first_any,
    second_any,
    inputs_any,
    win_any,
    wout_any,
    wlocal_any,
    wmix_any,
    cos_any,
    sin_any,
    joined_ref,
    weights_ref,
    target_ref,
    mask_ref,
    first_ref,
    second_ref,
    inputs_ref,
    win_ref,
    wout_ref,
    wlocal_ref,
    wmix_ref,
    cos_ref,
    sin_ref,
    feat_ext,
    act_ext,
    loss_ext,
    pre_ext,
    slope_first,
    hole_ref,
    first_adj,
    second_adj,
    grad_feat,
    strip_ref,
    spatial_out,
    spatial_in,
    grad_out,
    grad_in,
    back_out,
    back_in,
    col_cos,
    col_sin,
    col_cos_t,
    col_sin_t,
    held,
    slope_mix,
    win_double,
    wout_double,
    wmix_mixed,
    load_sems,
    halo_send,
    halo_recv,
    strip_send,
    strip_recv,
    send_sems,
    recv_sems,
):
    rows, cols, height, width, chunks, tile_rows, tile_cols, channels, edge = sizes
    devices = rows * cols
    half_width = chunks * 64
    lanes = chunks * 128
    freqs = width // 2
    col_factor = 1.0 / math.sqrt(width)
    row_factor = 1.0 / math.sqrt(height)
    my_row = lax.axis_index("row")
    my_col = lax.axis_index("col")
    me = my_row * cols + my_col
    barrier = pltpu.get_barrier_semaphore()

    def peer_of(step):
        return lax.rem(me + lax.rem(step * 77, devices), devices)

    def place(peer):
        return {"row": lax.div(peer, cols), "col": lax.rem(peer, cols)}

    def greet(step, carry):
        pl.semaphore_signal(barrier, inc=1, device_id=place(peer_of(step)), device_id_type=MESH)
        return carry

    lax.fori_loop(1, devices, greet, 0)

    center = (slice(4, 4 + tile_rows), slice(edge, edge + tile_cols))
    loads = [
        pltpu.make_async_copy(source, target, load_sems.at[index])
        for index, (source, target) in enumerate(
            [
                (win_any, win_ref),
                (inputs_any, inputs_ref),
                (cos_any, cos_ref),
                (sin_any, sin_ref),
                (first_any, first_ref),
                (second_any, second_ref),
                (features_any, feat_ext.at[pl.ds(4, tile_rows), pl.ds(edge, tile_cols)]),
                (wout_any, wout_ref),
                (wmix_any, wmix_ref),
                (mask_any, mask_ref),
                (target_any, target_ref),
                (wlocal_any, wlocal_ref),
            ]
        )
    ]
    for load in loads:
        load.start()

    def region(side, extent, thick, offset):
        if side < 0:
            return (offset, thick)
        if side > 0:
            return (offset + extent - thick, thick)
        return (offset, extent)

    def landing(side, extent, thick):
        if side < 0:
            return (extent + thick, thick)
        if side > 0:
            return (0, thick)
        return (thick, extent)

    def halo_copy(stage, side, source, target, thick, row_offset, col_offset):
        index = SIDES.index(side)
        source_rows = region(side[0], tile_rows, thick, row_offset)
        source_cols = region(side[1], tile_cols, edge, col_offset)
        target_rows = landing(side[0], tile_rows, thick)
        target_cols = landing(side[1], tile_cols, edge)
        return pltpu.make_async_remote_copy(
            src_ref=source.at[pl.ds(*source_rows), pl.ds(*source_cols)],
            dst_ref=target.at[pl.ds(*target_rows), pl.ds(*target_cols)],
            send_sem=halo_send.at[stage, index],
            recv_sem=halo_recv.at[stage, index],
            device_id={
                "row": lax.rem(my_row + side[0] + rows, rows),
                "col": lax.rem(my_col + side[1] + cols, cols),
            },
            device_id_type=MESH,
        )

    def clear_rows(ext, thick):
        @pl.when(my_row == 0)
        def _():
            ext[0:thick] = jnp.zeros_like(ext[0:thick])

        @pl.when(my_row == rows - 1)
        def _():
            ext[thick + tile_rows :] = jnp.zeros_like(ext[thick + tile_rows :])

    def clear_cols(ext):
        @pl.when(my_col == 0)
        def _():
            ext[:, 0:edge] = jnp.zeros_like(ext[:, 0:edge])

        @pl.when(my_col == cols - 1)
        def _():
            ext[:, edge + tile_cols :] = jnp.zeros_like(ext[:, edge + tile_cols :])

    def conv_rows(ext, pieces, first_col, count, kernel):
        taps = []
        for a in range(3):
            for b in range(3):
                parts = [
                    ext[start + 2 * a : start + 2 * a + n, first_col + 2 * b : first_col + 2 * b + count, :]
                    for start, n in pieces
                ]
                joint = parts[0] if len(parts) == 1 else jnp.concatenate(parts, axis=0)
                taps.append(joint.reshape(joint.shape[0] * count, channels))
        return dot(jnp.concatenate(taps, axis=1), kernel[...])

    even_row = ids((2 * freqs, 128), 0) % 2 == 0
    low_lane = ids((2 * freqs, 128), 1) < 64

    def column_forward(target):
        for j in range(chunks):
            piece = slice(j * 128, (j + 1) * 128)
            both = jnp.concatenate([held[0, :, piece], held[1, :, piece]], axis=1)
            cosine = dot(col_cos[...], both)
            sine = dot(col_sin[...], both)
            first = jnp.where(low_lane, cosine[:, :128], sine[:, :128])
            second = jnp.where(low_lane, cosine[:, 128:], sine[:, 128:])
            mixed_rows = (jnp.where(even_row, first, second) * col_factor).astype(jnp.bfloat16)
            target[j] = mixed_rows.reshape(freqs, 2, 128)

    def messages(source, target, index):
        def send(step, carry):
            peer = peer_of(step)
            pltpu.make_async_remote_copy(
                src_ref=source.at[:, peer],
                dst_ref=target.at[:, me],
                send_sem=send_sems.at[index],
                recv_sem=recv_sems.at[index],
                device_id=place(peer),
                device_id_type=MESH,
            ).start()
            return carry

        lax.fori_loop(1, devices, send, 0)
        pltpu.make_async_copy(source.at[:, me], target.at[:, me], recv_sems.at[index]).start()

    def arrived(target, index):
        pltpu.make_async_copy(target, target, recv_sems.at[index]).wait()

    def sent(source, index):
        rest = source.at[:, pl.ds(0, devices - 1)]
        pltpu.make_async_copy(rest, rest, send_sems.at[index]).wait()

    def row_transform(source, way):
        sign = jnp.where(ids((height, 128), 1) < 64, way, -way)
        results = []
        for j in range(chunks):
            cosine = dot(cos_ref[...], source[j])
            sine = dot(sin_ref[...], source[j])
            results.append((cosine + pltpu.roll(sine, 64, 1) * sign) * row_factor)
        return results

    pl.semaphore_wait(barrier, devices - 1)
    features_out = [halo_copy(0, side, features_any, feat_ext, 4, 0, 0) for side in SIDES]
    for copy in features_out:
        copy.start()

    loads[0].wait()
    double = ones_where(ids((half_width, lanes), 0) == 64 * (ids((half_width, lanes), 1) // 128) + ids((half_width, lanes), 1) % 64)
    win_double[...] = dot(win_ref[...], double).astype(jnp.bfloat16)
    loads[1].wait()
    for i in range(2):
        held[i] = dot(inputs_ref[i], win_double[...]).astype(jnp.bfloat16)
    loads[2].wait()
    loads[3].wait()
    pick = ones_where(ids((2 * freqs, freqs), 0) // 2 == ids((2 * freqs, freqs), 1))
    pick_t = ones_where(ids((freqs, 2 * freqs), 1) // 2 == ids((freqs, 2 * freqs), 0))
    alternate = (1 - 2 * (ids((2 * freqs, width), 1) % 2)).astype(jnp.float32)
    alternate_t = (1 - 2 * (ids((width, 2 * freqs), 0) % 2)).astype(jnp.float32)
    col_cos[...] = dot(pick, cos_ref[:freqs, :]).astype(jnp.bfloat16)
    col_sin[...] = jnp.where(ids((2 * freqs, width), 0) < 2, alternate, -dot(pick, sin_ref[:freqs, :])).astype(jnp.bfloat16)
    column_forward(spatial_out)
    messages(spatial_out, spatial_in, 0)
    loads[4].wait()
    for index in (6, 7):
        features_out[index].wait_recv()
    loads[6].wait()
    clear_cols(feat_ext.at[pl.ds(4, tile_rows)])

    wide = tile_cols + edge
    margin = edge // 2

    def first_conv(start):
        pre = conv_rows(feat_ext, [(start, 4)], edge - margin - 2, wide, first_ref)
        gate = jax.nn.sigmoid(pre)
        act = (pre * gate).reshape(4, wide, channels)
        row_id = my_row * tile_rows - 2 + start + ids((4, wide, channels), 0)
        col_id = my_col * tile_cols - margin + ids((4, wide, channels), 1)
        inside = (row_id >= 0) & (row_id < height) & (col_id >= 0) & (col_id < width)
        act_ext[start : start + 4, edge - margin : edge - margin + wide, :] = jnp.where(inside, act, 0.0).astype(jnp.bfloat16)
        slope = (gate * (1.0 + pre * (1.0 - gate))).reshape(4, wide, channels)
        low, high = max(start, 2), min(start + 4, 2 + tile_rows)
        slope_first[low - 2 : high - 2] = slope[low - start : high - start, margin : margin + tile_cols, :]

    first_conv(4)

    loads[5].wait()
    eye = ones_where(ids((channels, channels), 0) == ids((channels, channels), 1))
    for source, target in ((first_ref, first_adj), (second_ref, second_adj)):
        for tap in range(9):
            block = source[(8 - tap) * channels : (9 - tap) * channels, :]
            target[tap * channels : (tap + 1) * channels, :] = dot_t(eye, block).astype(jnp.bfloat16)
    loads[9].wait()
    spot = ids((tile_cols, tile_cols), 0) == ids((tile_cols, tile_cols), 1)
    for p in range(tile_rows):
        line = mask_ref[p : p + 1, :].astype(jnp.float32)
        spread = jnp.where(spot, line, 0.0).astype(jnp.bfloat16)
        hole_ref[p] = 1.0 + 2.0 * dot(spread, jnp.ones((tile_cols, channels), jnp.bfloat16))
    for copy in features_out[:6]:
        copy.wait_recv()
    clear_rows(feat_ext, 4)
    clear_cols(feat_ext)
    first_conv(0)
    first_conv(8)

    outer = [(0, 2), (tile_rows - 2, 2)]
    inner = [(2, tile_rows - 4)]

    def store(ext, pieces, value, thick):
        at = 0
        for start, n in pieces:
            ext[start + thick : start + thick + n, edge : edge + tile_cols, :] = value[at : at + n]
            at += n

    def gather(ref, pieces):
        parts = [ref[start : start + n] for start, n in pieces]
        return parts[0] if len(parts) == 1 else jnp.concatenate(parts, axis=0)

    def second_conv(pieces):
        pre = conv_rows(act_ext, pieces, edge - 2, tile_cols, second_ref)
        pre = pre.reshape(pre.shape[0] // tile_cols, tile_cols, channels)
        loss = gather(hole_ref, pieces) * (pre - gather(target_ref, pieces).astype(jnp.float32))
        store(loss_ext, pieces, loss.astype(jnp.bfloat16), 2)

    loads[10].wait()
    loss_out = [halo_copy(1, side, loss_ext, loss_ext, 2, 2, edge) for side in SIDES]
    second_conv(outer)
    for copy in loss_out[:6]:
        copy.start()
    second_conv(inner)
    for copy in loss_out[6:]:
        copy.start()
    for copy in loss_out[6:]:
        copy.wait_recv()
    clear_cols(loss_ext.at[pl.ds(2, tile_rows)])

    def third_conv(pieces):
        value = conv_rows(loss_ext, pieces, edge - 2, tile_cols, second_adj)
        value = value.reshape(value.shape[0] // tile_cols, tile_cols, channels) * gather(slope_first, pieces)
        store(pre_ext, pieces, value.astype(jnp.bfloat16), 2)

    third_conv(inner)
    for copy in loss_out[:6]:
        copy.wait_recv()
    clear_rows(loss_ext, 2)
    clear_cols(loss_ext)
    pre_out = [halo_copy(2, side, pre_ext, pre_ext, 2, 2, edge) for side in SIDES]
    third_conv(outer)
    for copy in pre_out:
        copy.start()

    col_cos_t[...] = dot(cos_ref[:, :freqs], pick_t).astype(jnp.bfloat16)
    col_sin_t[...] = jnp.where(ids((width, 2 * freqs), 1) < 2, alternate_t, -dot(sin_ref[:, :freqs], pick_t)).astype(jnp.bfloat16)
    loads[7].wait()
    double_t = ones_where(ids((lanes, half_width), 1) == 64 * (ids((lanes, half_width), 0) // 128) + ids((lanes, half_width), 0) % 64)
    wout_double[...] = dot(double_t, wout_ref[...]).astype(jnp.bfloat16)

    def place_of(lane):
        return ((lane % 128) // 64) * half_width + 64 * (lane // 128) + lane % 64

    order = ones_where(ids((lanes, lanes), 0) == place_of(ids((lanes, lanes), 1)))
    order_t = ones_where(ids((lanes, lanes), 1) == place_of(ids((lanes, lanes), 0)))
    loads[8].wait()
    partly = dot(order_t, wmix_ref[...]).astype(jnp.bfloat16)
    wmix_mixed[...] = dot(partly, order).astype(jnp.bfloat16)
    loads[11].wait()
    low_half = ids((win_double.shape[0], lanes), 1) % 128 < 64
    weights_ref[:, :lanes] = jnp.where(low_half, win_double[...].astype(jnp.float32), 0.0).astype(jnp.bfloat16)
    weights_ref[:, lanes:] = wlocal_ref[...]

    for copy in pre_out[6:]:
        copy.wait_recv()
    clear_cols(pre_ext.at[pl.ds(2, tile_rows)])

    def fourth_conv(pieces):
        value = conv_rows(pre_ext, pieces, edge - 2, tile_cols, first_adj).astype(jnp.bfloat16)
        value = value.reshape(value.shape[0] // tile_cols, tile_cols, channels)
        at = 0
        for start, n in pieces:
            grad_feat[start : start + n] = value[at : at + n]
            at += n

    def strip_send_to(hop):
        peer_col = lax.rem(my_col + hop, cols)
        return pltpu.make_async_remote_copy(
            src_ref=grad_feat.at[pl.ds(2 * peer_col, 2)],
            dst_ref=strip_ref.at[:, pl.ds(pl.multiple_of(my_col * tile_cols, tile_cols), tile_cols)],
            send_sem=strip_send.at[hop],
            recv_sem=strip_recv.at[hop],
            device_id={"row": my_row, "col": peer_col},
            device_id_type=MESH,
        )

    fourth_conv(inner)
    for copy in pre_out[:6]:
        copy.wait_recv()
    clear_rows(pre_ext, 2)
    clear_cols(pre_ext)
    fourth_conv(outer)
    strips_out = [strip_send_to(hop) for hop in range(1, cols)]
    for copy in strips_out:
        copy.start()
    own_strip = pltpu.make_async_copy(
        grad_feat.at[pl.ds(2 * my_col, 2)],
        strip_ref.at[:, pl.ds(pl.multiple_of(my_col * tile_cols, tile_cols), tile_cols)],
        strip_recv.at[0],
    )
    own_strip.start()

    arrived(spatial_in, 0)
    freq = row_transform([spatial_in[j].reshape(height, 128) for j in range(chunks)], 1.0)
    pre_mix = dot(jnp.concatenate(freq, axis=1).astype(jnp.bfloat16), wmix_mixed[...])
    gate = jax.nn.sigmoid(pre_mix)
    slope_mix[...] = gate * (1.0 + pre_mix * (1.0 - gate))

    own_strip.wait()
    for copy in strips_out:
        copy.wait_recv()
    for i in range(2):
        held[i] = dot_t(strip_ref[i], wout_double[...]).astype(jnp.bfloat16)
    column_forward(grad_out)
    messages(grad_out, grad_in, 1)
    joined_ref[:, :, lanes:] = strip_ref[...]
    arrived(grad_in, 1)
    freq = row_transform([grad_in[j].reshape(height, 128) for j in range(chunks)], 1.0)
    grad_mix = (jnp.concatenate(freq, axis=1) * slope_mix[...]).astype(jnp.bfloat16)
    mixed = dot_t(grad_mix, wmix_mixed[...]).astype(jnp.bfloat16)
    back = row_transform([mixed[:, j * 128 : (j + 1) * 128] for j in range(chunks)], -1.0)
    for j in range(chunks):
        back_out[j] = back[j].astype(jnp.bfloat16).reshape(devices, 2, 128)
    messages(back_out, back_in, 2)
    for copy in features_out + loss_out + pre_out + strips_out:
        copy.wait_send()
    sent(spatial_out, 0)
    sent(grad_out, 1)
    arrived(back_in, 2)
    keep = ids((width, 128), 1) < 64
    for j in range(chunks):
        block = back_in[j].reshape(2 * freqs, 128).astype(jnp.float32)
        both = jnp.concatenate([jnp.where(even_row, block, 0.0), jnp.where(even_row, 0.0, block)], axis=1)
        both = both.astype(jnp.bfloat16)
        cosine = dot(col_cos_t[...], both)
        sine = dot(col_sin_t[...], both)
        for i in range(2):
            piece = slice(i * 128, (i + 1) * 128)
            total = (cosine[:, piece] + pltpu.roll(sine[:, piece], 64, 1)) * col_factor
            joined_ref[i, :, j * 128 : (j + 1) * 128] = jnp.where(keep, total, 0.0).astype(jnp.bfloat16)
    sent(back_out, 2)


def shards(
    features,
    target,
    hole_mask,
    kernel_first,
    kernel_second,
    inputs,
    weight_in,
    weight_out,
    weight_local,
    weight_mix,
):
    rows, cols = lax.axis_size("row"), lax.axis_size("col")
    devices = rows * cols
    tile_rows, tile_cols, channels = features.shape
    width = inputs.shape[1]
    height = inputs.shape[0] * devices
    depth = inputs.shape[2]
    chunks = weight_in.shape[1] // 64
    lanes = chunks * 128
    edge = min(16, tile_cols)
    cos_table, sin_table = host_tables(width)
    wide = tile_cols + 2 * edge
    bf16, f32 = jnp.bfloat16, jnp.float32
    operands = (
        features,
        target,
        hole_mask,
        kernel_first.reshape(9 * channels, channels),
        kernel_second.reshape(9 * channels, channels),
        inputs,
        weight_in,
        weight_out,
        weight_local,
        weight_mix,
        jnp.asarray(cos_table),
        jnp.asarray(sin_table),
    )
    exchange = pltpu.VMEM((chunks, devices, 2, 128), bf16)
    table = pltpu.VMEM((width, width), bf16)
    kernel_shape = pltpu.VMEM((9 * channels, channels), bf16)
    vmem = pl.BlockSpec(memory_space=pltpu.VMEM)
    joined, weights = pl.pallas_call(
        functools.partial(
            block_kernel, (rows, cols, height, width, chunks, tile_rows, tile_cols, channels, edge)
        ),
        out_shape=(
            jax.ShapeDtypeStruct((2, width, lanes + channels), bf16),
            jax.ShapeDtypeStruct((depth, lanes + channels), bf16),
        ),
        in_specs=[pl.BlockSpec(memory_space=pl.ANY)] * len(operands),
        out_specs=(vmem, vmem),
        scratch_shapes=[pltpu.VMEM(item.shape, item.dtype) for item in operands[1:]]
        + [
            pltpu.VMEM((tile_rows + 8, wide, channels), bf16),
            pltpu.VMEM((tile_rows + 4, wide, channels), bf16),
            pltpu.VMEM((tile_rows + 4, wide, channels), bf16),
            pltpu.VMEM((tile_rows + 4, wide, channels), bf16),
            pltpu.VMEM((tile_rows, tile_cols, channels), f32),
            pltpu.VMEM((tile_rows, tile_cols, channels), f32),
            kernel_shape,
            kernel_shape,
            pltpu.VMEM((tile_rows, tile_cols, channels), bf16),
            pltpu.VMEM((2, width, channels), bf16),
        ]
        + [exchange] * 6
        + [table] * 4
        + [
            pltpu.VMEM((2, width, lanes), bf16),
            pltpu.VMEM((height, lanes), f32),
            pltpu.VMEM((depth, lanes), bf16),
            pltpu.VMEM((lanes, channels), bf16),
            pltpu.VMEM((lanes, lanes), bf16),
            pltpu.SemaphoreType.DMA((len(operands),)),
            pltpu.SemaphoreType.DMA((3, 8)),
            pltpu.SemaphoreType.DMA((3, 8)),
            pltpu.SemaphoreType.DMA((cols,)),
            pltpu.SemaphoreType.DMA((cols,)),
            pltpu.SemaphoreType.DMA((3,)),
            pltpu.SemaphoreType.DMA((3,)),
        ],
        compiler_params=pltpu.CompilerParams(
            collective_id=0, has_side_effects=True, vmem_limit_bytes=56 * 2**20
        ),
        name="block",
    )(*operands)
    total = jnp.einsum("rwc,fc->rwf", joined, weights, preferred_element_type=f32)
    return total.astype(bf16)


def solution(mesh):
    in_specs = (
        P("row", "col", None),
        P("row", "col", None),
        P("row", "col"),
        P(),
        P(),
        P(("row", "col"), None, None),
        P(),
        P(),
        P(),
        P(),
    )
    out_specs = P(("row", "col"), None, None)
    return jax.shard_map(shards, mesh=mesh, in_specs=in_specs, out_specs=out_specs, check_vma=False)
```

profile of v0, /device:TPU:1, one launch (start us, length us, event | category | flops | bytes accessed | tf_op | source)
XLA Modules:
  0.0 113.8 jit_solution(4005099759025077717)
XLA Ops:
  0.0 1.8 %copy.13.win_any = bf16[512,192]{1,0:T(8,128)(2,1)} copy(bf16[512,192]{0,1:T(8,128)(2,1)} %param.18) | data formatting | bytes 393216 | tf_op args[6]
  1.8 108.5 %block.1 = (bf16[2,512,640]{2,1,0:T(8,128)(2,1)}, bf16[512,640]{1,0:T(8,128)(2,1)}) custom-call(bf16[8,128,256]{2,1,0:T(8,128)(2,1)} %features_any.1, bf16[8,128,256]{2,1,0:T(8,128)(2,1)} %target_any.1, s32[8,128]{1,0:T(8,128)} %mask_any.1, bf16[2304,256]{1,0:T(8,128)(2,1)} %bitcast.6, bf16[2304,256]{1,0:T(8,128)(2,1)} %bitcast.7, ...), custom_call_target="tpu_custom_call" | custom-call | tf_op jit(solution)/shard_map/block/pallas_call | solution.py:503
  110.3 3.5 %convolution_convert_fusion = bf16[2,512,512]{2,1,0:T(8,128)(2,1)} fusion(bf16[2,512,640]{2,1,0:T(8,128)(2,1)} %get-tuple-element.7, bf16[512,640]{1,0:T(8,128)(2,1)} %get-tuple-element.8), kind=kOutput, calls=%fused_computation | convolution fusion | flops 671612928 | bytes 3014656 | tf_op jit(solution)/shard_map/rwc,fc->rwf/dot_general | solution.py:547
where the time goes:
time: 114 us
  Pallas kernels  109 us (96%)
  matrix products  3.46 us (3%)
  local copies, waits for them, and re-layouts  1.77 us (2%)
    pallas_call x1, Pallas kernels, shards(): pl.pallas_call(functools.partial(block_kernel, (rows, cols, height, width...  109 us
    dot_general x1, matrix products, shards(): jnp.einsum('rwc,fc->rwf', joined, weights, preferred_element_type=f32)  3.46 us

commit v1 on v0

--- a/solution.py
+++ b/solution.py
@@ -10,7 +10,8 @@
 from jax.sharding import PartitionSpec as P
 
 MESH = pl.DeviceIdType.MESH
-SIDES = [(-1, 0), (1, 0), (-1, -1), (-1, 1), (1, -1), (1, 1), (0, -1), (0, 1)]
+SIDES = [(0, -1), (0, 1), (-1, 0), (1, 0), (-1, -1), (-1, 1), (1, -1), (1, 1)]
+UNROLL = 8
 
 
 def host_tables(length):
@@ -107,19 +108,26 @@
     me = my_row * cols + my_col
     barrier = pltpu.get_barrier_semaphore()
 
-    def peer_of(step):
-        return lax.rem(me + lax.rem(step * 77, devices), devices)
-
-    def place(peer):
-        return {"row": lax.div(peer, cols), "col": lax.rem(peer, cols)}
-
-    def greet(step, carry):
-        pl.semaphore_signal(barrier, inc=1, device_id=place(peer_of(step)), device_id_type=MESH)
-        return carry
-
-    lax.fori_loop(1, devices, greet, 0)
-
-    center = (slice(4, 4 + tile_rows), slice(edge, edge + tile_cols))
+    def each_peer(action, low=0, high=cols):
+        for hop in range(low, high):
+            col = lax.rem(my_col + hop, cols)
+            per_turn = math.gcd(UNROLL, rows)
+
+            def turn(index, carry, hop=hop, col=col):
+                for k in range(per_turn):
+                    action(lax.rem(my_row + (index * per_turn + k) * 21, rows), col)
+                return carry
+
+            if hop == 0:
+                for k in range(1, per_turn):
+                    action(lax.rem(my_row + k * 21, rows), col)
+            lax.fori_loop(1 if hop == 0 else 0, rows // per_turn, turn, 0)
+
+    def greet(row, col):
+        pl.semaphore_signal(barrier, inc=1, device_id={"row": row, "col": col}, device_id_type=MESH)
+
+    each_peer(greet)
+
     loads = [
         pltpu.make_async_copy(source, target, load_sems.at[index])
         for index, (source, target) in enumerate(
@@ -174,6 +182,22 @@
             device_id_type=MESH,
         )
 
+    def exists(side, way):
+        row, col = my_row + way * side[0], my_col + way * side[1]
+        return (row >= 0) & (row < rows) & (col >= 0) & (col < cols)
+
+    def begin(copies, indices):
+        for index in indices:
+            pl.when(exists(SIDES[index], 1))(copies[index].start)
+
+    def receive(copies, indices):
+        for index in indices:
+            pl.when(exists(SIDES[index], -1))(copies[index].wait_recv)
+
+    def flush(copies):
+        for index in range(8):
+            pl.when(exists(SIDES[index], 1))(copies[index].wait_send)
+
     def clear_rows(ext, thick):
         @pl.when(my_row == 0)
         def _():
@@ -204,6 +228,10 @@
                 taps.append(joint.reshape(joint.shape[0] * count, channels))
         return dot(jnp.concatenate(taps, axis=1), kernel[...])
 
+    for ext, thick in ((feat_ext, 4), (loss_ext, 2), (pre_ext, 2)):
+        clear_rows(ext, thick)
+        clear_cols(ext)
+
     even_row = ids((2 * freqs, 128), 0) % 2 == 0
     low_lane = ids((2 * freqs, 128), 1) < 64
 
@@ -218,21 +246,20 @@
             mixed_rows = (jnp.where(even_row, first, second) * col_factor).astype(jnp.bfloat16)
             target[j] = mixed_rows.reshape(freqs, 2, 128)
 
-    def messages(source, target, index):
-        def send(step, carry):
-            peer = peer_of(step)
+    def messages(source, target, index, low=0, high=cols):
+        def send(row, col):
             pltpu.make_async_remote_copy(
-                src_ref=source.at[:, peer],
+                src_ref=source.at[:, row * cols + col],
                 dst_ref=target.at[:, me],
                 send_sem=send_sems.at[index],
                 recv_sem=recv_sems.at[index],
-                device_id=place(peer),
+                device_id={"row": row, "col": col},
                 device_id_type=MESH,
             ).start()
-            return carry
-
-        lax.fori_loop(1, devices, send, 0)
-        pltpu.make_async_copy(source.at[:, me], target.at[:, me], recv_sems.at[index]).start()
+
+        each_peer(send, low, high)
+        if low == 0:
+            pltpu.make_async_copy(source.at[:, me], target.at[:, me], recv_sems.at[index]).start()
 
     def arrived(target, index):
         pltpu.make_async_copy(target, target, recv_sems.at[index]).wait()
@@ -252,15 +279,14 @@
 
     pl.semaphore_wait(barrier, devices - 1)
     features_out = [halo_copy(0, side, features_any, feat_ext, 4, 0, 0) for side in SIDES]
-    for copy in features_out:
-        copy.start()
+    begin(features_out, range(8))
 
     loads[0].wait()
-    double = ones_where(ids((half_width, lanes), 0) == 64 * (ids((half_width, lanes), 1) // 128) + ids((half_width, lanes), 1) % 64)
-    win_double[...] = dot(win_ref[...], double).astype(jnp.bfloat16)
+    double_t = ones_where(ids((lanes, half_width), 1) == 64 * (ids((lanes, half_width), 0) // 128) + ids((lanes, half_width), 0) % 64)
+    win_double[...] = dot(double_t, win_ref[...]).astype(jnp.bfloat16)
     loads[1].wait()
     for i in range(2):
-        held[i] = dot(inputs_ref[i], win_double[...]).astype(jnp.bfloat16)
+        held[i] = dot_t(inputs_ref[i], win_double[...]).astype(jnp.bfloat16)
     loads[2].wait()
     loads[3].wait()
     pick = ones_where(ids((2 * freqs, freqs), 0) // 2 == ids((2 * freqs, freqs), 1))
@@ -270,12 +296,9 @@
     col_cos[...] = dot(pick, cos_ref[:freqs, :]).astype(jnp.bfloat16)
     col_sin[...] = jnp.where(ids((2 * freqs, width), 0) < 2, alternate, -dot(pick, sin_ref[:freqs, :])).astype(jnp.bfloat16)
     column_forward(spatial_out)
-    messages(spatial_out, spatial_in, 0)
     loads[4].wait()
-    for index in (6, 7):
-        features_out[index].wait_recv()
+    receive(features_out, (0, 1))
     loads[6].wait()
-    clear_cols(feat_ext.at[pl.ds(4, tile_rows)])
 
     wide = tile_cols + edge
     margin = edge // 2
@@ -306,10 +329,8 @@
         line = mask_ref[p : p + 1, :].astype(jnp.float32)
         spread = jnp.where(spot, line, 0.0).astype(jnp.bfloat16)
         hole_ref[p] = 1.0 + 2.0 * dot(spread, jnp.ones((tile_cols, channels), jnp.bfloat16))
-    for copy in features_out[:6]:
-        copy.wait_recv()
-    clear_rows(feat_ext, 4)
-    clear_cols(feat_ext)
+    receive(features_out, range(2, 8))
+    messages(spatial_out, spatial_in, 0, 0, 1)
     first_conv(0)
     first_conv(8)
 
@@ -335,14 +356,10 @@
     loads[10].wait()
     loss_out = [halo_copy(1, side, loss_ext, loss_ext, 2, 2, edge) for side in SIDES]
     second_conv(outer)
-    for copy in loss_out[:6]:
-        copy.start()
+    begin(loss_out, range(2, 8))
     second_conv(inner)
-    for copy in loss_out[6:]:
-        copy.start()
-    for copy in loss_out[6:]:
-        copy.wait_recv()
-    clear_cols(loss_ext.at[pl.ds(2, tile_rows)])
+    begin(loss_out, (0, 1))
+    receive(loss_out, (0, 1))
 
     def third_conv(pieces):
         value = conv_rows(loss_ext, pieces, edge - 2, tile_cols, second_adj)
@@ -350,19 +367,15 @@
         store(pre_ext, pieces, value.astype(jnp.bfloat16), 2)
 
     third_conv(inner)
-    for copy in loss_out[:6]:
-        copy.wait_recv()
-    clear_rows(loss_ext, 2)
-    clear_cols(loss_ext)
+    receive(loss_out, range(2, 8))
+    messages(spatial_out, spatial_in, 0, 1, 2)
     pre_out = [halo_copy(2, side, pre_ext, pre_ext, 2, 2, edge) for side in SIDES]
     third_conv(outer)
-    for copy in pre_out:
-        copy.start()
+    begin(pre_out, range(8))
 
     col_cos_t[...] = dot(cos_ref[:, :freqs], pick_t).astype(jnp.bfloat16)
     col_sin_t[...] = jnp.where(ids((width, 2 * freqs), 1) < 2, alternate_t, -dot(sin_ref[:, :freqs], pick_t)).astype(jnp.bfloat16)
     loads[7].wait()
-    double_t = ones_where(ids((lanes, half_width), 1) == 64 * (ids((lanes, half_width), 0) // 128) + ids((lanes, half_width), 0) % 64)
     wout_double[...] = dot(double_t, wout_ref[...]).astype(jnp.bfloat16)
 
     def place_of(lane):
@@ -374,13 +387,10 @@
     partly = dot(order_t, wmix_ref[...]).astype(jnp.bfloat16)
     wmix_mixed[...] = dot(partly, order).astype(jnp.bfloat16)
     loads[11].wait()
-    low_half = ids((win_double.shape[0], lanes), 1) % 128 < 64
-    weights_ref[:, :lanes] = jnp.where(low_half, win_double[...].astype(jnp.float32), 0.0).astype(jnp.bfloat16)
-    weights_ref[:, lanes:] = wlocal_ref[...]
-
-    for copy in pre_out[6:]:
-        copy.wait_recv()
-    clear_cols(pre_ext.at[pl.ds(2, tile_rows)])
+    low_half = ids(win_double.shape, 0) % 128 < 64
+    weights_ref[:lanes, :] = jnp.where(low_half, win_double[...].astype(jnp.float32), 0.0).astype(jnp.bfloat16)
+    weights_ref[lanes:, :] = dot_t(eye, wlocal_ref[...]).astype(jnp.bfloat16)
+    receive(pre_out, (0, 1))
 
     def fourth_conv(pieces):
         value = conv_rows(pre_ext, pieces, edge - 2, tile_cols, first_adj).astype(jnp.bfloat16)
@@ -390,32 +400,46 @@
             grad_feat[start : start + n] = value[at : at + n]
             at += n
 
-    def strip_send_to(hop):
-        peer_col = lax.rem(my_col + hop, cols)
+    here = pl.ds(pl.multiple_of(my_col * tile_cols, tile_cols), tile_cols)
+
+    def strip_copy(peer_col):
         return pltpu.make_async_remote_copy(
             src_ref=grad_feat.at[pl.ds(2 * peer_col, 2)],
-            dst_ref=strip_ref.at[:, pl.ds(pl.multiple_of(my_col * tile_cols, tile_cols), tile_cols)],
-            send_sem=strip_send.at[hop],
-            recv_sem=strip_recv.at[hop],
+            dst_ref=strip_ref.at[:, here],
+            send_sem=strip_send.at[peer_col],
+            recv_sem=strip_recv.at[my_col],
             device_id={"row": my_row, "col": peer_col},
             device_id_type=MESH,
         )
 
+    def strip_own():
+        return pltpu.make_async_copy(
+            grad_feat.at[pl.ds(2 * my_col, 2)], strip_ref.at[:, here], strip_recv.at[my_col]
+        )
+
+    def strip_begin(peer_cols):
+        for peer_col in peer_cols:
+            pl.when(my_col != peer_col)(strip_copy(peer_col).start)
+            pl.when(my_col == peer_col)(strip_own().start)
+
+    def strip_receive():
+        for peer_col in range(cols):
+            part = strip_ref.at[:, pl.ds(peer_col * tile_cols, tile_cols)]
+            pltpu.make_async_copy(part, part, strip_recv.at[peer_col]).wait()
+
     fourth_conv(inner)
-    for copy in pre_out[:6]:
-        copy.wait_recv()
-    clear_rows(pre_ext, 2)
-    clear_cols(pre_ext)
+    strip_begin(range(1, cols - 1))
+    receive(pre_out, range(2, 8))
+    messages(spatial_out, spatial_in, 0, 2, cols)
     fourth_conv(outer)
-    strips_out = [strip_send_to(hop) for hop in range(1, cols)]
-    for copy in strips_out:
-        copy.start()
-    own_strip = pltpu.make_async_copy(
-        grad_feat.at[pl.ds(2 * my_col, 2)],
-        strip_ref.at[:, pl.ds(pl.multiple_of(my_col * tile_cols, tile_cols), tile_cols)],
-        strip_recv.at[0],
-    )
-    own_strip.start()
+    strip_begin((0, cols - 1))
+
+    strip_receive()
+    for i in range(2):
+        held[i] = dot_t(strip_ref[i], wout_double[...]).astype(jnp.bfloat16)
+    column_forward(grad_out)
+    messages(grad_out, grad_in, 1)
+    joined_ref[:, :, lanes:] = strip_ref[...]
 
     arrived(spatial_in, 0)
     freq = row_transform([spatial_in[j].reshape(height, 128) for j in range(chunks)], 1.0)
@@ -423,14 +447,6 @@
     gate = jax.nn.sigmoid(pre_mix)
     slope_mix[...] = gate * (1.0 + pre_mix * (1.0 - gate))
 
-    own_strip.wait()
-    for copy in strips_out:
-        copy.wait_recv()
-    for i in range(2):
-        held[i] = dot_t(strip_ref[i], wout_double[...]).astype(jnp.bfloat16)
-    column_forward(grad_out)
-    messages(grad_out, grad_in, 1)
-    joined_ref[:, :, lanes:] = strip_ref[...]
     arrived(grad_in, 1)
     freq = row_transform([grad_in[j].reshape(height, 128) for j in range(chunks)], 1.0)
     grad_mix = (jnp.concatenate(freq, axis=1) * slope_mix[...]).astype(jnp.bfloat16)
@@ -439,8 +455,10 @@
     for j in range(chunks):
         back_out[j] = back[j].astype(jnp.bfloat16).reshape(devices, 2, 128)
     messages(back_out, back_in, 2)
-    for copy in features_out + loss_out + pre_out + strips_out:
-        copy.wait_send()
+    for copies in (features_out, loss_out, pre_out):
+        flush(copies)
+    for peer_col in range(cols):
+        pl.when(my_col != peer_col)(strip_copy(peer_col).wait_send)
     sent(spatial_out, 0)
     sent(grad_out, 1)
     arrived(back_in, 2)
@@ -489,7 +507,7 @@
         kernel_first.reshape(9 * channels, channels),
         kernel_second.reshape(9 * channels, channels),
         inputs,
-        weight_in,
+        weight_in.T,
         weight_out,
         weight_local,
         weight_mix,
@@ -506,7 +524,7 @@
         ),
         out_shape=(
             jax.ShapeDtypeStruct((2, width, lanes + channels), bf16),
-            jax.ShapeDtypeStruct((depth, lanes + channels), bf16),
+            jax.ShapeDtypeStruct((lanes + channels, depth), bf16),
         ),
         in_specs=[pl.BlockSpec(memory_space=pl.ANY)] * len(operands),
         out_specs=(vmem, vmem),
@@ -528,7 +546,7 @@
         + [
             pltpu.VMEM((2, width, lanes), bf16),
             pltpu.VMEM((height, lanes), f32),
-            pltpu.VMEM((depth, lanes), bf16),
+            pltpu.VMEM((lanes, depth), bf16),
             pltpu.VMEM((lanes, channels), bf16),
             pltpu.VMEM((lanes, lanes), bf16),
             pltpu.SemaphoreType.DMA((len(operands),)),
@@ -544,7 +562,7 @@
         ),
         name="block",
     )(*operands)
-    total = jnp.einsum("rwc,fc->rwf", joined, weights, preferred_element_type=f32)
+    total = jnp.einsum("rwc,cf->rwf", joined, weights, preferred_element_type=f32)
     return total.astype(bf16)
 
 

time: 114 us -> 104 us (0.912)
  Pallas kernels: 109 us -> 100 us
  local copies, waits for them, and re-layouts: 1.77 us -> 0 us
    pallas_call x1, Pallas kernels: 109 us -> 100 us  [shards(): pl.pallas_call(functools.partial(block_kernel, (rows, cols, height, width...]
    unnamed x1 -> x0, local copies, waits for them, and re-layouts: 1.77 us -> none
where the time goes in v1:
time: 104 us
  Pallas kernels  100 us (96%)
  matrix products  3.43 us (3%)
    pallas_call x1, Pallas kernels, shards(): pl.pallas_call(functools.partial(block_kernel, (rows, cols, height, width...  100 us
    dot_general x1, matrix products, shards(): jnp.einsum('rwc,cf->rwf', joined, weights, preferred_element_type=f32)  3.43 us

profile of v1, /device:TPU:1, one launch (start us, length us, event | category | flops | bytes accessed | tf_op | source)
XLA Modules:
  0.0 103.9 jit_solution(15220938945566257340)
XLA Ops:
  0.0 100.4 %block.1 = (bf16[2,512,640]{2,1,0:T(8,128)(2,1)}, bf16[640,512]{1,0:T(8,128)(2,1)}) custom-call(bf16[8,128,256]{2,1,0:T(8,128)(2,1)} %features_any.1, bf16[8,128,256]{2,1,0:T(8,128)(2,1)} %target_any.1, s32[8,128]{1,0:T(8,128)} %mask_any.1, bf16[2304,256]{1,0:T(8,128)(2,1)} %bitcast.7, bf16[2304,256]{1,0:T(8,128)(2,1)} %bitcast.8, ...), custom_call_target="tpu_custom_call" | custom-call | tf_op jit(solution)/shard_map/block/pallas_call | solution.py:521
  100.4 3.4 %convolution_convert_fusion = bf16[2,512,512]{2,1,0:T(8,128)(2,1)} fusion(bf16[2,512,640]{2,1,0:T(8,128)(2,1)} %get-tuple-element.7, bf16[640,512]{1,0:T(8,128)(2,1)} %get-tuple-element.8), kind=kOutput, calls=%fused_computation | convolution fusion | flops 671612928 | bytes 3014656 | tf_op jit(solution)/shard_map/rwc,cf->rwf/dot_general | solution.py:565

commit v2 on v1

--- a/solution.py
+++ b/solution.py
@@ -50,8 +50,7 @@
     wmix_any,
     cos_any,
     sin_any,
-    joined_ref,
-    weights_ref,
+    out_ref,
     target_ref,
     mask_ref,
     first_ref,
@@ -88,6 +87,7 @@
     win_double,
     wout_double,
     wmix_mixed,
+    grad_local,
     load_sems,
     halo_send,
     halo_recv,
@@ -217,16 +217,17 @@
             ext[:, edge + tile_cols :] = jnp.zeros_like(ext[:, edge + tile_cols :])
 
     def conv_rows(ext, pieces, first_col, count, kernel):
-        taps = []
-        for a in range(3):
-            for b in range(3):
-                parts = [
-                    ext[start + 2 * a : start + 2 * a + n, first_col + 2 * b : first_col + 2 * b + count, :]
-                    for start, n in pieces
+        results = []
+        for start, n in pieces:
+            for row in range(start, start + n, 2):
+                taps = [
+                    ext[row + 2 * a : row + 2 * a + 2, first_col + 2 * b : first_col + 2 * b + count, :]
+                    for a in range(3)
+                    for b in range(3)
                 ]
-                joint = parts[0] if len(parts) == 1 else jnp.concatenate(parts, axis=0)
-                taps.append(joint.reshape(joint.shape[0] * count, channels))
-        return dot(jnp.concatenate(taps, axis=1), kernel[...])
+                joint = jnp.concatenate([tap.reshape(2 * count, channels) for tap in taps], axis=1)
+                results.append((row, dot(joint, kernel[...]).reshape(2, count, channels)))
+        return results
 
     for ext, thick in ((feat_ext, 4), (loss_ext, 2), (pre_ext, 2)):
         clear_rows(ext, thick)
@@ -304,16 +305,17 @@
     margin = edge // 2
 
     def first_conv(start):
-        pre = conv_rows(feat_ext, [(start, 4)], edge - margin - 2, wide, first_ref)
-        gate = jax.nn.sigmoid(pre)
-        act = (pre * gate).reshape(4, wide, channels)
-        row_id = my_row * tile_rows - 2 + start + ids((4, wide, channels), 0)
-        col_id = my_col * tile_cols - margin + ids((4, wide, channels), 1)
-        inside = (row_id >= 0) & (row_id < height) & (col_id >= 0) & (col_id < width)
-        act_ext[start : start + 4, edge - margin : edge - margin + wide, :] = jnp.where(inside, act, 0.0).astype(jnp.bfloat16)
-        slope = (gate * (1.0 + pre * (1.0 - gate))).reshape(4, wide, channels)
-        low, high = max(start, 2), min(start + 4, 2 + tile_rows)
-        slope_first[low - 2 : high - 2] = slope[low - start : high - start, margin : margin + tile_cols, :]
+        shape = (2, wide, channels)
+        for row, pre in conv_rows(feat_ext, [(start, 4)], edge - margin - 2, wide, first_ref):
+            gate = jax.nn.sigmoid(pre)
+            row_id = my_row * tile_rows - 2 + row + ids(shape, 0)
+            col_id = my_col * tile_cols - margin + ids(shape, 1)
+            inside = (row_id >= 0) & (row_id < height) & (col_id >= 0) & (col_id < width)
+            act = jnp.where(inside, pre * gate, 0.0).astype(jnp.bfloat16)
+            act_ext[row : row + 2, edge - margin : edge - margin + wide, :] = act
+            if 2 <= row < 2 + tile_rows:
+                slope = gate * (1.0 + pre * (1.0 - gate))
+                slope_first[row - 2 : row] = slope[:, margin : margin + tile_cols, :]
 
     first_conv(4)
 
@@ -337,21 +339,12 @@
     outer = [(0, 2), (tile_rows - 2, 2)]
     inner = [(2, tile_rows - 4)]
 
-    def store(ext, pieces, value, thick):
-        at = 0
-        for start, n in pieces:
-            ext[start + thick : start + thick + n, edge : edge + tile_cols, :] = value[at : at + n]
-            at += n
-
-    def gather(ref, pieces):
-        parts = [ref[start : start + n] for start, n in pieces]
-        return parts[0] if len(parts) == 1 else jnp.concatenate(parts, axis=0)
+    body = slice(edge, edge + tile_cols)
 
     def second_conv(pieces):
-        pre = conv_rows(act_ext, pieces, edge - 2, tile_cols, second_ref)
-        pre = pre.reshape(pre.shape[0] // tile_cols, tile_cols, channels)
-        loss = gather(hole_ref, pieces) * (pre - gather(target_ref, pieces).astype(jnp.float32))
-        store(loss_ext, pieces, loss.astype(jnp.bfloat16), 2)
+        for row, pre in conv_rows(act_ext, pieces, edge - 2, tile_cols, second_ref):
+            loss = hole_ref[row : row + 2] * (pre - target_ref[row : row + 2].astype(jnp.float32))
+            loss_ext[row + 2 : row + 4, body, :] = loss.astype(jnp.bfloat16)
 
     loads[10].wait()
     loss_out = [halo_copy(1, side, loss_ext, loss_ext, 2, 2, edge) for side in SIDES]
@@ -362,9 +355,8 @@
     receive(loss_out, (0, 1))
 
     def third_conv(pieces):
-        value = conv_rows(loss_ext, pieces, edge - 2, tile_cols, second_adj)
-        value = value.reshape(value.shape[0] // tile_cols, tile_cols, channels) * gather(slope_first, pieces)
-        store(pre_ext, pieces, value.astype(jnp.bfloat16), 2)
+        for row, value in conv_rows(loss_ext, pieces, edge - 2, tile_cols, second_adj):
+            pre_ext[row + 2 : row + 4, body, :] = (value * slope_first[row : row + 2]).astype(jnp.bfloat16)
 
     third_conv(inner)
     receive(loss_out, range(2, 8))
@@ -388,17 +380,12 @@
     wmix_mixed[...] = dot(partly, order).astype(jnp.bfloat16)
     loads[11].wait()
     low_half = ids(win_double.shape, 0) % 128 < 64
-    weights_ref[:lanes, :] = jnp.where(low_half, win_double[...].astype(jnp.float32), 0.0).astype(jnp.bfloat16)
-    weights_ref[lanes:, :] = dot_t(eye, wlocal_ref[...]).astype(jnp.bfloat16)
+    win_double[...] = jnp.where(low_half, win_double[...].astype(jnp.float32), 0.0).astype(jnp.bfloat16)
     receive(pre_out, (0, 1))
 
     def fourth_conv(pieces):
-        value = conv_rows(pre_ext, pieces, edge - 2, tile_cols, first_adj).astype(jnp.bfloat16)
-        value = value.reshape(value.shape[0] // tile_cols, tile_cols, channels)
-        at = 0
-        for start, n in pieces:
-            grad_feat[start : start + n] = value[at : at + n]
-            at += n
+        for row, value in conv_rows(pre_ext, pieces, edge - 2, tile_cols, first_adj):
+            grad_feat[row : row + 2] = value.astype(jnp.bfloat16)
 
     here = pl.ds(pl.multiple_of(my_col * tile_cols, tile_cols), tile_cols)
 
@@ -439,7 +426,6 @@
         held[i] = dot_t(strip_ref[i], wout_double[...]).astype(jnp.bfloat16)
     column_forward(grad_out)
     messages(grad_out, grad_in, 1)
-    joined_ref[:, :, lanes:] = strip_ref[...]
 
     arrived(spatial_in, 0)
     freq = row_transform([spatial_in[j].reshape(height, 128) for j in range(chunks)], 1.0)
@@ -461,6 +447,8 @@
         pl.when(my_col != peer_col)(strip_copy(peer_col).wait_send)
     sent(spatial_out, 0)
     sent(grad_out, 1)
+    for i in range(2):
+        grad_local[i] = dot_t(strip_ref[i], wlocal_ref[...])
     arrived(back_in, 2)
     keep = ids((width, 128), 1) < 64
     for j in range(chunks):
@@ -472,7 +460,9 @@
         for i in range(2):
             piece = slice(i * 128, (i + 1) * 128)
             total = (cosine[:, piece] + pltpu.roll(sine[:, piece], 64, 1)) * col_factor
-            joined_ref[i, :, j * 128 : (j + 1) * 128] = jnp.where(keep, total, 0.0).astype(jnp.bfloat16)
+            held[i, :, j * 128 : (j + 1) * 128] = jnp.where(keep, total, 0.0).astype(jnp.bfloat16)
+    for i in range(2):
+        out_ref[i] = (dot(held[i], win_double[...]) + grad_local[i]).astype(jnp.bfloat16)
     sent(back_out, 2)
 
 
@@ -518,16 +508,13 @@
     table = pltpu.VMEM((width, width), bf16)
     kernel_shape = pltpu.VMEM((9 * channels, channels), bf16)
     vmem = pl.BlockSpec(memory_space=pltpu.VMEM)
-    joined, weights = pl.pallas_call(
+    return pl.pallas_call(
         functools.partial(
             block_kernel, (rows, cols, height, width, chunks, tile_rows, tile_cols, channels, edge)
         ),
-        out_shape=(
-            jax.ShapeDtypeStruct((2, width, lanes + channels), bf16),
-            jax.ShapeDtypeStruct((lanes + channels, depth), bf16),
-        ),
+        out_shape=jax.ShapeDtypeStruct((2, width, depth), bf16),
         in_specs=[pl.BlockSpec(memory_space=pl.ANY)] * len(operands),
-        out_specs=(vmem, vmem),
+        out_specs=vmem,
         scratch_shapes=[pltpu.VMEM(item.shape, item.dtype) for item in operands[1:]]
         + [
             pltpu.VMEM((tile_rows + 8, wide, channels), bf16),
@@ -549,6 +536,7 @@
             pltpu.VMEM((lanes, depth), bf16),
             pltpu.VMEM((lanes, channels), bf16),
             pltpu.VMEM((lanes, lanes), bf16),
+            pltpu.VMEM((2, width, depth), f32),
             pltpu.SemaphoreType.DMA((len(operands),)),
             pltpu.SemaphoreType.DMA((3, 8)),
             pltpu.SemaphoreType.DMA((3, 8)),
@@ -562,8 +550,6 @@
         ),
         name="block",
     )(*operands)
-    total = jnp.einsum("rwc,cf->rwf", joined, weights, preferred_element_type=f32)
-    return total.astype(bf16)
 
 
 def solution(mesh):

time: 104 us -> 102 us (0.981)
  matrix products: 3.43 us -> 0 us
  local copies, waits for them, and re-layouts: 0 us -> 2.26 us
    dot_general x1 -> x0, matrix products: 3.43 us -> none  [shards(): jnp.einsum('rwc,cf->rwf', joined, weights, preferred_element_type=f32)]
    unnamed x0 -> x1, local copies, waits for them, and re-layouts: none -> 2.26 us
where the time goes in v2:
time: 102 us
  Pallas kernels  100 us (98%)
  local copies, waits for them, and re-layouts  2.26 us (2%)
    pallas_call x1, Pallas kernels, shards(): pl.pallas_call(functools.partial(block_kernel, (rows, cols, height, width...  100 us
    unnamed x1, local copies, waits for them, and re-layouts  2.26 us

profile of v2, /device:TPU:1, one launch (start us, length us, event | category | flops | bytes accessed | tf_op | source)
XLA Modules:
  0.0 102.3 jit_solution(9501525332828011818)
XLA Ops:
  0.0 100.0 %block.1 = bf16[2,512,512]{2,1,0:T(8,128)(2,1)} custom-call(bf16[8,128,256]{2,1,0:T(8,128)(2,1)} %features_any.1, bf16[8,128,256]{2,1,0:T(8,128)(2,1)} %target_any.1, s32[8,128]{1,0:T(8,128)} %mask_any.1, bf16[2304,256]{1,0:T(8,128)(2,1)} %bitcast.3, bf16[2304,256]{1,0:T(8,128)(2,1)} %bitcast.4, bf16[2,512,512]{2,1,0:T(8,128)(2,1)} %inputs_any.1, ...), custom_call_target="tpu_custom_call" | custom-call | tf_op jit(solution)/shard_map/block/pallas_call | solution.py:511
  100.1 2.3 %copy.14 = bf16[2,512,512]{2,1,0:T(8,128)(2,1)} copy(bf16[2,512,512]{2,1,0:T(8,128)(2,1)} %block.1) | data formatting | bytes 2097152

commit v3 on v2

--- a/solution.py
+++ b/solution.py
@@ -88,6 +88,10 @@
     wout_double,
     wmix_mixed,
     grad_local,
+    relay_feat,
+    relay_loss,
+    relay_pre,
+    relay_sems,
     load_sems,
     halo_send,
     halo_recv,
@@ -164,12 +168,20 @@
             return (0, thick)
         return (thick, extent)
 
-    def halo_copy(stage, side, source, target, thick, row_offset, col_offset):
+    group = 4 if rows % 16 == 0 else 2
+    split = tile_cols * 5 // 8
+    rest = tile_cols - split
+    in_group = lax.rem(my_row, group)
+    at_first, at_last = in_group == 0, in_group == group - 1
+
+    def halo_copy(stage, side, source, target, thick, row_offset, col_offset, part=False):
         index = SIDES.index(side)
         source_rows = region(side[0], tile_rows, thick, row_offset)
         source_cols = region(side[1], tile_cols, edge, col_offset)
         target_rows = landing(side[0], tile_rows, thick)
         target_cols = landing(side[1], tile_cols, edge)
+        if part:
+            source_cols, target_cols = (col_offset, split), (edge, split)
         return pltpu.make_async_remote_copy(
             src_ref=source.at[pl.ds(*source_rows), pl.ds(*source_cols)],
             dst_ref=target.at[pl.ds(*target_rows), pl.ds(*target_cols)],
@@ -186,17 +198,81 @@
         row, col = my_row + way * side[0], my_col + way * side[1]
         return (row >= 0) & (row < rows) & (col >= 0) & (col < cols)
 
-    def begin(copies, indices):
-        for index in indices:
-            pl.when(exists(SIDES[index], 1))(copies[index].start)
-
-    def receive(copies, indices):
-        for index in indices:
-            pl.when(exists(SIDES[index], -1))(copies[index].wait_recv)
-
-    def flush(copies):
-        for index in range(8):
-            pl.when(exists(SIDES[index], 1))(copies[index].wait_send)
+    class Exchange:
+        def __init__(self, stage, source, target, thick, row_offset, col_offset, buffer):
+            common = (source, target, thick, row_offset, col_offset)
+            self.whole = [halo_copy(stage, side, *common) for side in SIDES]
+            self.part = {index: halo_copy(stage, SIDES[index], *common, part=True) for index in (2, 3)}
+
+            def hop(row_start, distance):
+                return pltpu.make_async_remote_copy(
+                    src_ref=source.at[pl.ds(row_start, thick), pl.ds(col_offset + split, rest)],
+                    dst_ref=buffer,
+                    send_sem=relay_sems.at[0, stage],
+                    recv_sem=relay_sems.at[1, stage],
+                    device_id={"row": lax.rem(my_row + distance + rows, rows), "col": my_col},
+                    device_id_type=MESH,
+                )
+
+            def onward(row_start, distance):
+                return pltpu.make_async_remote_copy(
+                    src_ref=buffer,
+                    dst_ref=target.at[pl.ds(row_start, thick), pl.ds(edge + split, rest)],
+                    send_sem=relay_sems.at[2, stage],
+                    recv_sem=relay_sems.at[3, stage],
+                    device_id={"row": lax.rem(my_row + distance + rows, rows), "col": my_col},
+                    device_id_type=MESH,
+                )
+
+            back, ahead = my_row >= group, my_row + group < rows
+            up = hop(row_offset, group - 1)
+            down = hop(row_offset + tile_rows - thick, 1 - group)
+            self.hops = [(at_first & back, up), (at_last & ahead, down)]
+            self.onwards = [
+                (at_first & ahead, onward(0, group)),
+                (at_last & back, onward(thick + tile_rows, -group)),
+            ]
+            self.finals = [
+                (at_first & back, onward(0, group)),
+                (at_last & ahead, onward(thick + tile_rows, -group)),
+            ]
+
+        def each(self, index, way, action):
+            there = exists(SIDES[index], way)
+            if index not in (2, 3):
+                pl.when(there)(getattr(self.whole[index], action))
+                return
+            far = at_first if (SIDES[index][0] < 0) == (way > 0) else at_last
+            pl.when(there & far)(getattr(self.part[index], action))
+            pl.when(there & jnp.logical_not(far))(getattr(self.whole[index], action))
+
+        def begin(self, indices):
+            if 2 in indices:
+                for there, copy in self.hops:
+                    pl.when(there)(copy.start)
+            for index in indices:
+                self.each(index, 1, "start")
+
+        def relay(self):
+            for there, copy in self.onwards:
+
+                @pl.when(there)
+                def _(copy=copy):
+                    self.hops[0][1].wait_recv()
+                    copy.start()
+
+        def receive(self, indices):
+            for index in indices:
+                self.each(index, -1, "wait_recv")
+            if 2 in indices:
+                for there, copy in self.finals:
+                    pl.when(there)(copy.wait_recv)
+
+        def flush(self):
+            for index in range(8):
+                self.each(index, 1, "wait_send")
+            for there, copy in self.hops + self.onwards:
+                pl.when(there)(copy.wait_send)
 
     def clear_rows(ext, thick):
         @pl.when(my_row == 0)
@@ -279,8 +355,8 @@
         return results
 
     pl.semaphore_wait(barrier, devices - 1)
-    features_out = [halo_copy(0, side, features_any, feat_ext, 4, 0, 0) for side in SIDES]
-    begin(features_out, range(8))
+    features_out = Exchange(0, features_any, feat_ext, 4, 0, 0, relay_feat)
+    features_out.begin(range(8))
 
     loads[0].wait()
     double_t = ones_where(ids((lanes, half_width), 1) == 64 * (ids((lanes, half_width), 0) // 128) + ids((lanes, half_width), 0) % 64)
@@ -298,7 +374,8 @@
     col_sin[...] = jnp.where(ids((2 * freqs, width), 0) < 2, alternate, -dot(pick, sin_ref[:freqs, :])).astype(jnp.bfloat16)
     column_forward(spatial_out)
     loads[4].wait()
-    receive(features_out, (0, 1))
+    features_out.receive((0, 1))
+    features_out.relay()
     loads[6].wait()
 
     wide = tile_cols + edge
@@ -331,7 +408,7 @@
         line = mask_ref[p : p + 1, :].astype(jnp.float32)
         spread = jnp.where(spot, line, 0.0).astype(jnp.bfloat16)
         hole_ref[p] = 1.0 + 2.0 * dot(spread, jnp.ones((tile_cols, channels), jnp.bfloat16))
-    receive(features_out, range(2, 8))
+    features_out.receive(range(2, 8))
     messages(spatial_out, spatial_in, 0, 0, 1)
     first_conv(0)
     first_conv(8)
@@ -347,23 +424,24 @@
             loss_ext[row + 2 : row + 4, body, :] = loss.astype(jnp.bfloat16)
 
     loads[10].wait()
-    loss_out = [halo_copy(1, side, loss_ext, loss_ext, 2, 2, edge) for side in SIDES]
+    loss_out = Exchange(1, loss_ext, loss_ext, 2, 2, edge, relay_loss)
     second_conv(outer)
-    begin(loss_out, range(2, 8))
+    loss_out.begin(range(2, 8))
     second_conv(inner)
-    begin(loss_out, (0, 1))
-    receive(loss_out, (0, 1))
+    loss_out.begin((0, 1))
+    loss_out.receive((0, 1))
+    loss_out.relay()
 
     def third_conv(pieces):
         for row, value in conv_rows(loss_ext, pieces, edge - 2, tile_cols, second_adj):
             pre_ext[row + 2 : row + 4, body, :] = (value * slope_first[row : row + 2]).astype(jnp.bfloat16)
 
     third_conv(inner)
-    receive(loss_out, range(2, 8))
+    loss_out.receive(range(2, 8))
     messages(spatial_out, spatial_in, 0, 1, 2)
-    pre_out = [halo_copy(2, side, pre_ext, pre_ext, 2, 2, edge) for side in SIDES]
+    pre_out = Exchange(2, pre_ext, pre_ext, 2, 2, edge, relay_pre)
     third_conv(outer)
-    begin(pre_out, range(8))
+    pre_out.begin(range(8))
 
     col_cos_t[...] = dot(cos_ref[:, :freqs], pick_t).astype(jnp.bfloat16)
     col_sin_t[...] = jnp.where(ids((width, 2 * freqs), 1) < 2, alternate_t, -dot(sin_ref[:, :freqs], pick_t)).astype(jnp.bfloat16)
@@ -381,7 +459,8 @@
     loads[11].wait()
     low_half = ids(win_double.shape, 0) % 128 < 64
     win_double[...] = jnp.where(low_half, win_double[...].astype(jnp.float32), 0.0).astype(jnp.bfloat16)
-    receive(pre_out, (0, 1))
+    pre_out.receive((0, 1))
+    pre_out.relay()
 
     def fourth_conv(pieces):
         for row, value in conv_rows(pre_ext, pieces, edge - 2, tile_cols, first_adj):
@@ -416,7 +495,7 @@
 
     fourth_conv(inner)
     strip_begin(range(1, cols - 1))
-    receive(pre_out, range(2, 8))
+    pre_out.receive(range(2, 8))
     messages(spatial_out, spatial_in, 0, 2, cols)
     fourth_conv(outer)
     strip_begin((0, cols - 1))
@@ -441,8 +520,8 @@
     for j in range(chunks):
         back_out[j] = back[j].astype(jnp.bfloat16).reshape(devices, 2, 128)
     messages(back_out, back_in, 2)
-    for copies in (features_out, loss_out, pre_out):
-        flush(copies)
+    for exchange in (features_out, loss_out, pre_out):
+        exchange.flush()
     for peer_col in range(cols):
         pl.when(my_col != peer_col)(strip_copy(peer_col).wait_send)
     sent(spatial_out, 0)
@@ -537,6 +616,10 @@
             pltpu.VMEM((lanes, channels), bf16),
             pltpu.VMEM((lanes, lanes), bf16),
             pltpu.VMEM((2, width, depth), f32),
+            pltpu.VMEM((4, tile_cols - tile_cols * 5 // 8, channels), bf16),
+            pltpu.VMEM((2, tile_cols - tile_cols * 5 // 8, channels), bf16),
+            pltpu.VMEM((2, tile_cols - tile_cols * 5 // 8, channels), bf16),
+            pltpu.SemaphoreType.DMA((4, 3)),
             pltpu.SemaphoreType.DMA((len(operands),)),
             pltpu.SemaphoreType.DMA((3, 8)),
             pltpu.SemaphoreType.DMA((3, 8)),

time: 102 us -> 94.7 us (0.928)
  Pallas kernels: 100 us -> 92.4 us
    pallas_call x1, Pallas kernels: 100 us -> 92.4 us  [shards(): pl.pallas_call(functools.partial(block_kernel, (rows, cols, height, width...]
where the time goes in v3:
time: 94.7 us; the launch traced here: 94.6 us
  Pallas kernels  92.4 us (98%)
  local copies, waits for them, and re-layouts  2.26 us (2%)
    pallas_call x1, Pallas kernels, shards(): pl.pallas_call(functools.partial(block_kernel, (rows, cols, height, width...  92.4 us
    unnamed x1, local copies, waits for them, and re-layouts  2.26 us

profile of v3, /device:TPU:1, one launch (start us, length us, event | category | flops | bytes accessed | tf_op | source)
XLA Modules:
  0.0 94.6 jit_solution(3393231241221132925)
XLA Ops:
  0.0 92.4 %block.1 = bf16[2,512,512]{2,1,0:T(8,128)(2,1)} custom-call(bf16[8,128,256]{2,1,0:T(8,128)(2,1)} %features_any.1, bf16[8,128,256]{2,1,0:T(8,128)(2,1)} %target_any.1, s32[8,128]{1,0:T(8,128)} %mask_any.1, bf16[2304,256]{1,0:T(8,128)(2,1)} %bitcast.3, bf16[2304,256]{1,0:T(8,128)(2,1)} %bitcast.4, bf16[2,512,512]{2,1,0:T(8,128)(2,1)} %inputs_any.1, ...), custom_call_target="tpu_custom_call" | custom-call | tf_op jit(solution)/shard_map/block/pallas_call | solution.py:590
  92.4 2.3 %copy.14 = bf16[2,512,512]{2,1,0:T(8,128)(2,1)} copy(bf16[2,512,512]{2,1,0:T(8,128)(2,1)} %block.1) | data formatting | bytes 2097152

commit v4 on v3

--- a/solution.py
+++ b/solution.py
@@ -11,7 +11,7 @@
 
 MESH = pl.DeviceIdType.MESH
 SIDES = [(0, -1), (0, 1), (-1, 0), (1, 0), (-1, -1), (-1, 1), (1, -1), (1, 1)]
-UNROLL = 8
+UNROLL = 16
 
 
 def host_tables(length):
@@ -117,14 +117,19 @@
             col = lax.rem(my_col + hop, cols)
             per_turn = math.gcd(UNROLL, rows)
 
-            def turn(index, carry, hop=hop, col=col):
+            def visit(base, k, col=col):
+                row = base + (k * 21) % rows
+                action(jnp.where(row >= rows, row - rows, row), col)
+
+            def turn(index, carry, visit=visit):
+                base = lax.rem(my_row + index * (per_turn * 21), rows)
                 for k in range(per_turn):
-                    action(lax.rem(my_row + (index * per_turn + k) * 21, rows), col)
+                    visit(base, k)
                 return carry
 
             if hop == 0:
                 for k in range(1, per_turn):
-                    action(lax.rem(my_row + k * 21, rows), col)
+                    visit(my_row, k)
             lax.fori_loop(1 if hop == 0 else 0, rows // per_turn, turn, 0)
 
     def greet(row, col):
@@ -345,14 +350,18 @@
         rest = source.at[:, pl.ds(0, devices - 1)]
         pltpu.make_async_copy(rest, rest, send_sems.at[index]).wait()
 
-    def row_transform(source, way):
+    def row_transform(signal, way):
         sign = jnp.where(ids((height, 128), 1) < 64, way, -way)
+        cosine = dot(cos_ref[...], signal)
+        sine = dot(sin_ref[...], signal)
         results = []
         for j in range(chunks):
-            cosine = dot(cos_ref[...], source[j])
-            sine = dot(sin_ref[...], source[j])
-            results.append((cosine + pltpu.roll(sine, 64, 1) * sign) * row_factor)
+            piece = slice(j * 128, (j + 1) * 128)
+            results.append((cosine[:, piece] + pltpu.roll(sine[:, piece], 64, 1) * sign) * row_factor)
         return results
+
+    def collected(source):
+        return jnp.concatenate([source[j].reshape(height, 128) for j in range(chunks)], axis=1)
 
     pl.semaphore_wait(barrier, devices - 1)
     features_out = Exchange(0, features_any, feat_ext, 4, 0, 0, relay_feat)
@@ -409,7 +418,6 @@
         spread = jnp.where(spot, line, 0.0).astype(jnp.bfloat16)
         hole_ref[p] = 1.0 + 2.0 * dot(spread, jnp.ones((tile_cols, channels), jnp.bfloat16))
     features_out.receive(range(2, 8))
-    messages(spatial_out, spatial_in, 0, 0, 1)
     first_conv(0)
     first_conv(8)
 
@@ -429,6 +437,7 @@
     loss_out.begin(range(2, 8))
     second_conv(inner)
     loss_out.begin((0, 1))
+    messages(spatial_out, spatial_in, 0, 0, 2)
     loss_out.receive((0, 1))
     loss_out.relay()
 
@@ -438,10 +447,10 @@
 
     third_conv(inner)
     loss_out.receive(range(2, 8))
-    messages(spatial_out, spatial_in, 0, 1, 2)
     pre_out = Exchange(2, pre_ext, pre_ext, 2, 2, edge, relay_pre)
     third_conv(outer)
     pre_out.begin(range(8))
+    messages(spatial_out, spatial_in, 0, 2, cols)
 
     col_cos_t[...] = dot(cos_ref[:, :freqs], pick_t).astype(jnp.bfloat16)
     col_sin_t[...] = jnp.where(ids((width, 2 * freqs), 1) < 2, alternate_t, -dot(sin_ref[:, :freqs], pick_t)).astype(jnp.bfloat16)
@@ -496,7 +505,6 @@
     fourth_conv(inner)
     strip_begin(range(1, cols - 1))
     pre_out.receive(range(2, 8))
-    messages(spatial_out, spatial_in, 0, 2, cols)
     fourth_conv(outer)
     strip_begin((0, cols - 1))
 
@@ -507,16 +515,16 @@
     messages(grad_out, grad_in, 1)
 
     arrived(spatial_in, 0)
-    freq = row_transform([spatial_in[j].reshape(height, 128) for j in range(chunks)], 1.0)
+    freq = row_transform(collected(spatial_in), 1.0)
     pre_mix = dot(jnp.concatenate(freq, axis=1).astype(jnp.bfloat16), wmix_mixed[...])
     gate = jax.nn.sigmoid(pre_mix)
     slope_mix[...] = gate * (1.0 + pre_mix * (1.0 - gate))
 
     arrived(grad_in, 1)
-    freq = row_transform([grad_in[j].reshape(height, 128) for j in range(chunks)], 1.0)
+    freq = row_transform(collected(grad_in), 1.0)
     grad_mix = (jnp.concatenate(freq, axis=1) * slope_mix[...]).astype(jnp.bfloat16)
     mixed = dot_t(grad_mix, wmix_mixed[...]).astype(jnp.bfloat16)
-    back = row_transform([mixed[:, j * 128 : (j + 1) * 128] for j in range(chunks)], -1.0)
+    back = row_transform(mixed, -1.0)
     for j in range(chunks):
         back_out[j] = back[j].astype(jnp.bfloat16).reshape(devices, 2, 128)
     messages(back_out, back_in, 2)

time: 94.7 us -> 91.8 us (0.969)
  Pallas kernels: 92.4 us -> 89.4 us
    pallas_call x1, Pallas kernels: 92.4 us -> 89.4 us  [shards(): pl.pallas_call(functools.partial(block_kernel, (rows, cols, height, width...]
where the time goes in v4:
time: 91.8 us; the launch traced here: 91.7 us
  Pallas kernels  89.4 us (97%)
  local copies, waits for them, and re-layouts  2.26 us (2%)
    pallas_call x1, Pallas kernels, shards(): pl.pallas_call(functools.partial(block_kernel, (rows, cols, height, width...  89.4 us
    unnamed x1, local copies, waits for them, and re-layouts  2.26 us

profile of v4, /device:TPU:1, one launch (start us, length us, event | category | flops | bytes accessed | tf_op | source)
XLA Modules:
  0.0 91.7 jit_solution(6157894867531115081)
XLA Ops:
  0.0 89.4 %block.1 = bf16[2,512,512]{2,1,0:T(8,128)(2,1)} custom-call(bf16[8,128,256]{2,1,0:T(8,128)(2,1)} %features_any.1, bf16[8,128,256]{2,1,0:T(8,128)(2,1)} %target_any.1, s32[8,128]{1,0:T(8,128)} %mask_any.1, bf16[2304,256]{1,0:T(8,128)(2,1)} %bitcast.3, bf16[2304,256]{1,0:T(8,128)(2,1)} %bitcast.4, bf16[2,512,512]{2,1,0:T(8,128)(2,1)} %inputs_any.1, ...), custom_call_target="tpu_custom_call" | custom-call | tf_op jit(solution)/shard_map/block/pallas_call | solution.py:598
  89.4 2.3 %copy.14 = bf16[2,512,512]{2,1,0:T(8,128)(2,1)} copy(bf16[2,512,512]{2,1,0:T(8,128)(2,1)} %block.1) | data formatting | bytes 2097152

commit v5 on v4

--- a/solution.py
+++ b/solution.py
@@ -11,7 +11,6 @@
 
 MESH = pl.DeviceIdType.MESH
 SIDES = [(0, -1), (0, 1), (-1, 0), (1, 0), (-1, -1), (-1, 1), (1, -1), (1, 1)]
-UNROLL = 16
 
 
 def host_tables(length):
@@ -112,25 +111,34 @@
     me = my_row * cols + my_col
     barrier = pltpu.get_barrier_semaphore()
 
+    near = min(4, rows)
+    mid = min(4, rows // near)
+    far = rows // (near * mid)
+
+    def by_distance(count):
+        return sorted(range(count), key=lambda step: -min(step, count - step))
+
     def each_peer(action, low=0, high=cols):
-        for hop in range(low, high):
-            col = lax.rem(my_col + hop, cols)
-            per_turn = math.gcd(UNROLL, rows)
-
-            def visit(base, k, col=col):
-                row = base + (k * 21) % rows
-                action(jnp.where(row >= rows, row - rows, row), col)
-
-            def turn(index, carry, visit=visit):
-                base = lax.rem(my_row + index * (per_turn * 21), rows)
-                for k in range(per_turn):
-                    visit(base, k)
-                return carry
-
-            if hop == 0:
-                for k in range(1, per_turn):
-                    visit(my_row, k)
-            lax.fori_loop(1 if hop == 0 else 0, rows // per_turn, turn, 0)
+        for step in by_distance(mid):
+            for hop in range(low, high):
+                col = lax.rem(my_col + hop, cols)
+                own = step == 0 and hop == 0
+
+                def visit(base, k, col=col):
+                    row = base + k
+                    action(jnp.where(row >= rows, row - rows, row), col)
+
+                def turn(index, carry, own=own, step=step, visit=visit):
+                    block = index if own else lax.rem(index + far // 2, far)
+                    base = lax.rem(my_row + step * near + block * (near * mid), rows)
+                    for k in by_distance(near):
+                        visit(base, k)
+                    return carry
+
+                lax.fori_loop(1 if own else 0, far, turn, 0)
+                if own:
+                    for k in range(1, near):
+                        visit(my_row, k)
 
     def greet(row, col):
         pl.semaphore_signal(barrier, inc=1, device_id={"row": row, "col": col}, device_id_type=MESH)

time: 91.8 us -> 92.6 us (level)
  no operation moved by 1% of the time
where the time goes in v5:
time: 92.6 us; the launch traced here: 92.5 us
  Pallas kernels  90.2 us (97%)
  local copies, waits for them, and re-layouts  2.26 us (2%)
    pallas_call x1, Pallas kernels, shards(): pl.pallas_call(functools.partial(block_kernel, (rows, cols, height, width...  90.2 us
    unnamed x1, local copies, waits for them, and re-layouts  2.26 us

profile of v5, /device:TPU:1, one launch (start us, length us, event | category | flops | bytes accessed | tf_op | source)
XLA Modules:
  0.0 92.5 jit_solution(186172940639810425)
XLA Ops:
  0.0 90.2 %block.1 = bf16[2,512,512]{2,1,0:T(8,128)(2,1)} custom-call(bf16[8,128,256]{2,1,0:T(8,128)(2,1)} %features_any.1, bf16[8,128,256]{2,1,0:T(8,128)(2,1)} %target_any.1, s32[8,128]{1,0:T(8,128)} %mask_any.1, bf16[2304,256]{1,0:T(8,128)(2,1)} %bitcast.3, bf16[2304,256]{1,0:T(8,128)(2,1)} %bitcast.4, bf16[2,512,512]{2,1,0:T(8,128)(2,1)} %inputs_any.1, ...), custom_call_target="tpu_custom_call" | custom-call | tf_op jit(solution)/shard_map/block/pallas_call | solution.py:606
  90.2 2.3 %copy.14 = bf16[2,512,512]{2,1,0:T(8,128)(2,1)} copy(bf16[2,512,512]{2,1,0:T(8,128)(2,1)} %block.1) | data formatting | bytes 2097152
